TPU v7x, 32 devices: a whole 2x2x4 slice. The times are simulated.
32 devices in a mesh: parts: 2 (over y), sub: 4 (over z), row: 2 (over x), col: 2 (over core).
Axes of the slice: x: 2, y: 2, z: 4, core: 2. Of those that a mesh axis runs over, the one named last changes fastest.
Arguments:
- loads: float32 [8, 32, 1024], P(('parts', 'sub'), 'col'), parts along dimension 0, may hold values from -6 to 6
- weights: float32 [8, 1024], P(('parts', 'sub')), parts along dimension 0, may hold values from 0.25 to 4
- dual_ops: bfloat16 [8, 2048, 2048], P(('parts', 'sub'), 'row'), parts along dimension 0, as said below
- corner_maps: bfloat16 [8, 24, 2048], P(('parts', 'sub'), None, 'row'), parts along dimension 0, may hold values from -0.25 to 0.25
- coarse_inverse: float32 [96, 48], P('parts'), parts along dimension 0, as said below
- corner_ids: int32 [8, 24], P('parts'), parts along dimension 0, may hold values from 0 to 47, as said below
- iface_sizes: int32 [8], P('parts'), parts along dimension 0, may hold values from 512 to 1024, as said below
- left_partner: int32 [8, 1024], P(('parts', 'sub')), parts along dimension 0, may hold values from 0 to 1023, as said below
- right_partner: int32 [8, 1024], P(('parts', 'sub')), parts along dimension 0, may hold values from 0 to 1023, as said below
Outputs:
- solution: float32 [8, 32, 1024], P(('parts', 'sub'), 'col'), parts along dimension 0
- residual: float32 [8, 32, 1024], P(('parts', 'sub'), 'col'), parts along dimension 0
There are 2 independent parts, one for each index of `parts`. A program takes and returns all parts, laid end to end along the dimension named above; each array names one. Nothing has to cross between parts.
Inputs may be any that keep to these rules, and one draw needn't show every extreme that they name: Global indices 24/2 * s to 24/2 * s + 24/2 - 1 are the corners of the interface between s and s+1; the first half of subdomain s's corner_ids is a permutation of those of interface s-1, the second half a permutation of those of interface s. `left_partner`: each row s is a permutation that maps the slots below iface_sizes[s-1] onto slots below it. `right_partner`: each row s is a permutation that maps the slots below iface_sizes[s] onto slots below it, and is the inverse of left_partner[s+1]. `dual_ops`: symmetric positive definite. `coarse_inverse`: symmetric positive definite. For each s < 2, one of iface_sizes[s] and iface_sizes[s + 2] is 896 or more and the other 640 or less.
All inputs are finite; a program needn't handle non-finite values.
Results may differ from a plain program's by a relative error of at most 0.015.
Values may be sent and summed in bfloat16 or wider, within the bound.
No kernel may reach another device: no remote copies, remote signals or barrier semaphores. Data moves between devices by JAX's collectives and lax.ppermute only.
A program may use at most 64 MiB of HBM per device.

v0:
```python
import jax
import jax.numpy as jnp
from jax import lax
from jax.sharding import PartitionSpec as P

TILE = 128
ITERS = 2


def shifted(value, axis, steps):
    count = lax.axis_size(axis)
    pairs = [(source, (source + steps) % count) for source in range(count)]
    return lax.ppermute(value, axis, pairs)


def inner(first, second, half):
    return jnp.sum(first[:, :half] * second[:, :half], axis=1)


def paired_totals(residual, precond, image, half):
    return lax.psum((inner(residual, precond, half), inner(precond, image, half)), "sub")


def tile_products(vector, rows_op, first_tile, last_tile, output):

    def one_tile(tile_at, acc):
        piece = lax.dynamic_slice_in_dim(rows_op, tile_at * TILE, TILE, 0)
        product = lax.dot_general(
            vector, piece, (((1,), (1,)), ((), ())), preferred_element_type=jnp.float32
        )
        return lax.dynamic_update_slice_in_dim(acc, product, tile_at * TILE, 1)

    return lax.fori_loop(first_tile, last_tile, one_tile, output)


def live_tiles(size_before, size_after, block_start, block, half):
    left_live = jnp.clip(size_before - block_start, 0, block)
    right_live = jnp.clip(size_after - (block_start - half), 0, block)
    live_cols = jnp.where(block_start < half, left_live, right_live)
    return (live_cols + TILE - 1) // TILE


def per_device(
    loads,
    weights,
    dual_ops,
    corner_maps,
    coarse_inverse,
    corner_ids,
    iface_sizes,
    left_partner,
    right_partner,
):
    half = loads.shape[2]
    block = dual_ops.shape[1]
    width = coarse_inverse.shape[0]
    subdomain = lax.axis_index("sub")
    count = lax.axis_size("sub")
    row_index = lax.axis_index("row")
    left_map = left_partner[0]
    right_map = right_partner[0]
    slots = jnp.arange(half, dtype=jnp.int32)
    size_before = iface_sizes[(subdomain + count - 1) % count]
    size_after = iface_sizes[subdomain]
    live_left = (slots < size_before).astype(jnp.float32)
    live_right = (right_map < size_after).astype(jnp.float32)
    columns = jnp.arange(width, dtype=jnp.int32)
    own_hot = (corner_ids[subdomain][:, None] == columns[None, :]).astype(jnp.float32)
    operator = dual_ops[0]
    coupling = corner_maps[0]
    block_start = row_index * block
    own_tiles = live_tiles(size_before, size_after, block_start, block, half)

    def apply_operator(vec):
        halfway = vec.astype(jnp.bfloat16)
        empty = jnp.zeros((halfway.shape[0], block), jnp.float32)
        local = tile_products(halfway, operator, jnp.int32(0), own_tiles, empty)
        own_slots = lax.dynamic_slice_in_dim(halfway, row_index * block, block, 1)
        corner = lax.dot_general(
            own_slots, coupling, (((1,), (1,)), ((), ())), preferred_element_type=jnp.float32
        )
        scattered = jnp.dot(corner, own_hot, precision=lax.Precision.HIGHEST)
        coarse = lax.psum(scattered, ("sub", "row"))
        solved = jnp.dot(coarse, coarse_inverse, precision=lax.Precision.HIGHEST)
        back = lax.dot_general(
            solved, own_hot, (((1,), (1,)), ((), ())), precision=lax.Precision.HIGHEST
        ).astype(jnp.bfloat16)
        united = local + jnp.dot(back, coupling, preferred_element_type=jnp.float32)
        whole = lax.all_gather(united.astype(jnp.bfloat16), "row", axis=1, tiled=True).astype(
            united.dtype
        )
        lower = whole[:, :half]
        upper = whole[:, half:]
        arrived_left = shifted(upper.astype(jnp.bfloat16), "sub", 1).astype(upper.dtype)
        arrived_right = shifted(lower.astype(jnp.bfloat16), "sub", -1).astype(lower.dtype)
        result_left = (lower + jnp.take(arrived_left, left_map, axis=1)) * live_left
        result_right = (upper + jnp.take(arrived_right, right_map, axis=1)) * live_right
        return jnp.concatenate([result_left, result_right], axis=1)

    received = (
        shifted(loads[0].astype(jnp.bfloat16), "sub", -1).astype(jnp.float32),
        shifted(weights.astype(jnp.bfloat16), "sub", -1).astype(weights.dtype),
    )
    right_load = jnp.take(received[0], right_map, axis=1) * live_right
    right_weight = jnp.take(received[1], right_map, axis=1)
    residual = jnp.concatenate([loads[0] * live_left, right_load], axis=1)
    scaling = jnp.concatenate([weights, right_weight], axis=1)
    solution = jnp.zeros_like(residual)
    precond = scaling * residual
    image = apply_operator(precond)
    gamma, delta = paired_totals(residual, precond, image, half)
    alpha = gamma / delta
    direction = precond
    along = image
    for step in range(ITERS):
        solution = solution + alpha[:, None] * direction
        residual = residual - alpha[:, None] * along
        if step + 1 < ITERS:
            precond = scaling * residual
            image = apply_operator(precond)
            gamma_next, delta = paired_totals(residual, precond, image, half)
            ratio = gamma_next / gamma
            alpha = gamma_next / (delta - ratio * gamma_next / alpha)
            direction = precond + ratio[:, None] * direction
            along = image + ratio[:, None] * along
            gamma = gamma_next
    return (solution[:, :half][None], residual[:, :half][None])


def solution(mesh):
    placed = (
        P(("parts", "sub"), "col", None),
        P(("parts", "sub"), None),
        P(("parts", "sub"), "row", None),
        P(("parts", "sub"), None, "row"),
        P("parts", None),
        P("parts", None),
        P("parts"),
        P(("parts", "sub"), None),
        P(("parts", "sub"), None),
    )
    return jax.shard_map(
        per_device,
        mesh=mesh,
        in_specs=placed,
        out_specs=(P(("parts", "sub"), "col", None), P(("parts", "sub"), "col", None)),
        check_vma=False,
    )
```

profile of v0, /device:TPU:0, one launch (start us, length us, event | category | flops | bytes accessed | tf_op | source)
XLA Modules:
  0.0 136.2 jit_solution(17909804324471528583)
XLA Ops:
  0.7 0.9 bitcast_convert_fusion
  1.5 5.1 %collective-permute-start.1 = (bf16[16,1024]{1,0:T(8,128)(2,1)S(1)}, bf16[16,1024]{1,0:T(8,128)(2,1)S(1)}, u32[]{:S(2)}, u32[]{:S(2)}) collective-permute-start(bf16[16,1024]{1,0:T(8,128)(2,1)S(1)} %bitcast_convert_fusion), channel_id=1, source_target_pairs={{0,12},{4,0},{8,4},{12,8},{1,13},{5,1},{9,5},{13,9},{2,14},{6,2},{... | collective-permute-start | bytes 98312 | tf_op jit(solution)/shard_map/ppermute | solution.py:13
  6.6 0.7 convert_element_type.71
  7.3 0.4 collective-permute-start
  7.8 0.7 compare_select_fusion
  8.4 0.7 fusion.36
  9.1 1.3 fusion.49
  10.5 1.3 fusion.35
  11.8 1.3 compare_convert_fusion
  13.1 0.8 bitcast_multiply_fusion.1
  14.0 0.7 fusion.40
  14.7 0.7 fusion.37
  16.7 4.5 %gather_fusion = f32[1024]{0:T(1024)S(1)} fusion(f32[1024]{0:T(1024)S(1)} %bitcast.80, s32[1024]{0:T(1024)S(1)} %broadcast_clamp_fusion), kind=kCustom, calls=%fused_computation.5 | custom fusion | bytes 12288 | tf_op jit(solution)/shard_map/jit(_take)/gather | solution.py:105
  21.4 0.1 copy.21
  21.5 2.8 %gather_fusion.1 = f32[1024,16]{1,0:T(8,128)S(1)} fusion(f32[16,1024]{0,1:T(8,128)S(1)} %copy.21, s32[1024]{0:T(1024)S(1)} %fusion.36), kind=kCustom, calls=%fused_computation.clone | custom fusion | bytes 135168 | tf_op jit(solution)/shard_map/jit(_take)/gather | solution.py:104
  24.3 0.2 copy.22
  24.5 10.4 %while.20 = (s32[]{:T(128)}, f32[16,1024]{1,0:T(8,128)S(1)}, s32[]{:T(128)}, bf16[1024,2048]{1,0:T(8,128)(2,1)}, bf16[16,2048]{1,0:T(8,128)(2,1)S(1)}, /*index=5*/s32[]{:T(128)}, s32[]{:T(128)}, s32[]{:T(128)}, s32[]{:T(128)}) while((s32[]{:T(128)}, f32[16,1024]{1,0:T(8,128)S(1)}, s32[]{:T(128)}, bf16[1024,2048]{1,0:T(8,128)(2,1)}, ...), condition=%wide.region_3.5_spmd, body=%wide.region_2.4_spmd.sunk | while | flops 8388614 | bytes 599179 | solution.py:33
  24.6 1.3 fusion.72
  25.9 1.3 fusion.72
  27.1 1.3 fusion.72
  28.4 1.3 fusion.72
  29.7 1.3 fusion.72
  31.0 1.3 fusion.72
  32.3 1.3 fusion.72
  33.6 1.3 fusion.72
  34.9 0.1 fusion.25
  35.1 0.2 fusion.30
  35.3 18.9 %psum.43 = f32[16,48]{1,0:T(8,128)S(1)} all-reduce(f32[16,48]{1,0:T(8,128)S(1)} %fusion.30), channel_id=1, replica_groups=mesh['parts'=2,'sub'=4,'row'=2,'col'=2] {'sub','row'}, use_global_device_ids=true, to_apply=%region_4.6 | all-reduce | flops 768 | bytes 6144 | tf_op jit(solution)/shard_map/psum | solution.py:83
  54.3 0.2 convolution_convert_fusion.1
  54.5 0.1 fusion.6
  54.6 4.6 %all_gather.6 = bf16[16,2048]{1,0:T(8,128)(2,1)S(1)} all-gather(bf16[16,1024]{1,0:T(8,128)(2,1)S(1)} %fusion.6), channel_id=1, replica_groups=mesh['parts'=2,'sub'=4,'row'=2,'col'=2] {'row'}, dimensions={1}, use_global_device_ids=true | all-gather | bytes 98304 | tf_op jit(solution)/shard_map/all_gather | solution.py:89
  59.2 3.8 %collective-permute-start.3 = (bf16[16,1024]{1,0:T(8,128)(2,1)S(1)}, bf16[16,1024]{1,0:T(8,128)(2,1)S(1)}, u32[]{:S(2)}, u32[]{:S(2)}) collective-permute-start(bf16[16,1024]{1,0:T(8,128)(2,1)S(1)} %get-tuple-element.103), channel_id=1, source_target_pairs={{0,12},{4,0},{8,4},{12,8},{1,13},{5,1},{9,5},{13,9},{2,14},{6,2},{... | collective-permute-start | bytes 98312 | tf_op jit(solution)/shard_map/ppermute | solution.py:13
  63.1 1.9 %collective-permute-done.2 = bf16[16,1024]{1,0:T(8,128)(2,1)S(1)} collective-permute-done((bf16[16,1024]{1,0:T(8,128)(2,1)S(1)}, bf16[16,1024]{1,0:T(8,128)(2,1)S(1)}, u32[]{:S(2)}, u32[]{:S(2)}) %collective-permute-start.2) | collective-permute-done | bytes 32800 | tf_op jit(solution)/shard_map/ppermute | solution.py:13
  65.1 2.8 %gather_fusion.2 = f32[1024,16]{1,0:T(8,128)S(1)} fusion(f32[16,1024]{0,1:T(8,128)S(1)} %copy.23, s32[1024]{0:T(1024)S(1)} %fusion.37), kind=kCustom, calls=%fused_computation.1.clone | custom fusion | bytes 135168 | tf_op jit(solution)/shard_map/jit(_take)/gather | solution.py:96
  67.9 0.2 copy.24
  68.1 0.1 copy.25
  68.2 2.8 %gather_fusion.3 = f32[1024,16]{1,0:T(8,128)S(1)} fusion(f32[16,1024]{0,1:T(8,128)S(1)} %copy.25, s32[1024]{0:T(1024)S(1)} %fusion.36), kind=kCustom, calls=%fused_computation.2.clone | custom fusion | bytes 135168 | tf_op jit(solution)/shard_map/jit(_take)/gather | solution.py:97
  71.0 0.2 copy.26
  71.2 0.1 multiply_reduce_fusion.2
  71.3 9.1 %all-reduce.1 = (f32[16]{0:T(128)S(1)}, f32[16]{0:T(128)S(1)}) all-reduce(f32[16]{0:T(128)S(1)} %get-tuple-element.64, f32[16]{0:T(128)S(1)} %get-tuple-element.63), channel_id=1, replica_groups=mesh['parts'=2,'sub'=4,'row'=2,'col'=2] {'sub'}, use_global_device_ids=true, to_apply=%region_1.3 | all-reduce | flops 32 | bytes 256 | tf_op jit(solution)/shard_map/psum | solution.py:21
  80.6 10.3 %while.21 = (s32[]{:T(128)}, f32[16,1024]{1,0:T(8,128)S(1)}, s32[]{:T(128)}, bf16[1024,2048]{1,0:T(8,128)(2,1)}, bf16[16,2048]{1,0:T(8,128)(2,1)S(1)}, /*index=5*/s32[]{:T(128)}, s32[]{:T(128)}, s32[]{:T(128)}, s32[]{:T(128)}) while((s32[]{:T(128)}, f32[16,1024]{1,0:T(8,128)S(1)}, s32[]{:T(128)}, bf16[1024,2048]{1,0:T(8,128)(2,1)}, ...), condition=%wide.region_10.12_spmd, body=%wide.region_9.11_spmd.sunk | while | flops 8388614 | bytes 599179 | solution.py:33
  80.6 1.3 fusion.75
  81.9 1.3 fusion.75
  83.2 1.3 fusion.75
  84.5 1.3 fusion.75
  85.8 1.3 fusion.75
  87.1 1.3 fusion.75
  88.4 1.3 fusion.75
  89.7 1.3 fusion.75
  91.0 0.2 fusion.29
  91.2 18.7 %psum.46 = f32[16,48]{1,0:T(8,128)S(1)} all-reduce(f32[16,48]{1,0:T(8,128)S(1)} %fusion.29), channel_id=1, replica_groups=mesh['parts'=2,'sub'=4,'row'=2,'col'=2] {'sub','row'}, use_global_device_ids=true, to_apply=%region_11.13 | all-reduce | flops 768 | bytes 6144 | tf_op jit(solution)/shard_map/psum | solution.py:83
  110.0 0.2 convolution_convert_fusion
  110.2 0.1 fusion.7
  110.3 4.6 %all_gather.7 = bf16[16,2048]{1,0:T(8,128)(2,1)S(1)} all-gather(bf16[16,1024]{1,0:T(8,128)(2,1)S(1)} %fusion.7), channel_id=1, replica_groups=mesh['parts'=2,'sub'=4,'row'=2,'col'=2] {'row'}, dimensions={1}, use_global_device_ids=true | all-gather | bytes 98304 | tf_op jit(solution)/shard_map/all_gather | solution.py:89
  114.9 2.0 %collective-permute-start.4 = (bf16[16,1024]{1,0:T(8,128)(2,1)S(1)}, bf16[16,1024]{1,0:T(8,128)(2,1)S(1)}, u32[]{:S(2)}, u32[]{:S(2)}) collective-permute-start(bf16[16,1024]{1,0:T(8,128)(2,1)S(1)} %get-tuple-element.101), channel_id=1, source_target_pairs={{0,4},{4,8},{8,12},{12,0},{1,5},{5,9},{9,13},{13,1},{2,6},{6,10},{... | collective-permute-start | bytes 98312 | tf_op jit(solution)/shard_map/ppermute | solution.py:13
  117.0 1.9 %collective-permute-done.5 = bf16[16,1024]{1,0:T(8,128)(2,1)S(1)} collective-permute-done((bf16[16,1024]{1,0:T(8,128)(2,1)S(1)}, bf16[16,1024]{1,0:T(8,128)(2,1)S(1)}, u32[]{:S(2)}, u32[]{:S(2)}) %collective-permute-start.5) | collective-permute-done | bytes 32800 | tf_op jit(solution)/shard_map/ppermute | solution.py:13
  119.0 2.8 %gather_fusion.5 = f32[1024,16]{1,0:T(8,128)S(1)} fusion(f32[16,1024]{0,1:T(8,128)S(1)} %copy.29, s32[1024]{0:T(1024)S(1)} %fusion.36), kind=kCustom, calls=%fused_computation.4.clone | custom fusion | bytes 135168 | tf_op jit(solution)/shard_map/jit(_take)/gather | solution.py:97
  121.8 0.2 copy.30
  122.0 0.1 copy.27
  122.1 2.8 %gather_fusion.4 = f32[1024,16]{1,0:T(8,128)S(1)} fusion(f32[16,1024]{0,1:T(8,128)S(1)} %copy.27, s32[1024]{0:T(1024)S(1)} %fusion.37), kind=kCustom, calls=%fused_computation.3.clone | custom fusion | bytes 135168 | tf_op jit(solution)/shard_map/jit(_take)/gather | solution.py:96
  124.9 0.2 copy.28
  125.1 0.1 multiply_reduce_fusion
  125.3 10.2 %all-reduce = (f32[16]{0:T(128)S(1)}, f32[16]{0:T(128)S(1)}) all-reduce(f32[16]{0:T(128)S(1)} %get-tuple-element.62, f32[16]{0:T(128)S(1)} %get-tuple-element.61), channel_id=1, replica_groups=mesh['parts'=2,'sub'=4,'row'=2,'col'=2] {'sub'}, use_global_device_ids=true, to_apply=%region_8.10 | all-reduce | flops 32 | bytes 256 | tf_op jit(solution)/shard_map/psum | solution.py:21
  135.4 0.7 fusion.16
  (39 shorter events, 1.0 us)
Async XLA Ops:
  0.6 34.3 %copy-start = (bf16[1,24,1024]{2,1,0:T(8,128)(2,1)S(1)}, bf16[1,24,1024]{2,1,0:T(8,128)(2,1)}, u32[]{:S(2)}) copy-start(bf16[1,24,1024]{2,1,0:T(8,128)(2,1)} %param.18) | copy-start | bytes 147460
  0.6 20.7 %copy-start.5 = (f32[1,1024]{1,0:T(1,128)S(1)}, f32[1,1024]{1,0:T(1,128)}, u32[]{:S(2)}) copy-start(f32[1,1024]{1,0:T(1,128)} %param.16) | copy-start | bytes 12292
  0.7 20.6 %copy-start.2 = (s32[1,1024]{1,0:T(1,128)S(1)}, s32[1,1024]{1,0:T(1,128)}, u32[]{:S(2)}) copy-start(s32[1,1024]{1,0:T(1,128)} %param.23) | copy-start | bytes 12292
  1.5 19.8 %collective-permute-start.1 = (bf16[16,1024]{1,0:T(8,128)(2,1)S(1)}, bf16[16,1024]{1,0:T(8,128)(2,1)S(1)}, u32[]{:S(2)}, u32[]{:S(2)}) collective-permute-start(bf16[16,1024]{1,0:T(8,128)(2,1)S(1)} %bitcast_convert_fusion), channel_id=1, source_target_pairs={{0,12},{4,0},{8,4},{12,8},{1,13},{5,1},{9,5},{13,9},{2,14},{6,2},{... | collective-permute-start | bytes 98312 | tf_op jit(solution)/shard_map/ppermute | solution.py:13
  7.3 9.4 %collective-permute-start = (bf16[1,1024]{1,0:T(2,128)(2,1)S(1)}, bf16[1,1024]{1,0:T(2,128)(2,1)S(1)}, u32[]{:S(2)}, u32[]{:S(2)}) collective-permute-start(bf16[1,1024]{1,0:T(2,128)(2,1)S(1)} %convert_element_type.71), channel_id=1, source_target_pairs={{0,12},{4,0},{8,4},{12,8},{1,13},{5,1},{9,5},{13,9},{2,14},{6,2},{... | collective-permute-start | bytes 6152 | tf_op jit(solution)/shard_map/ppermute | solution.py:13
  16.7 37.4 %copy-start.3 = (f32[48,48]{1,0:T(8,128)S(1)}, f32[48,48]{1,0:T(8,128)}, u32[]{:S(2)}) copy-start(f32[48,48]{1,0:T(8,128)} %param.19) | copy-start | bytes 27652
  16.7 46.3 %copy-start.4 = (s32[1,1024]{1,0:T(1,128)S(1)}, s32[1,1024]{1,0:T(1,128)}, u32[]{:S(2)}) copy-start(s32[1,1024]{1,0:T(1,128)} %param.22) | copy-start | bytes 12292
  24.5 46.7 %copy-start.1 = (f32[1,16,1024]{2,1,0:T(8,128)S(1)}, f32[1,16,1024]{2,1,0:T(8,128)}, u32[]{:S(2)}) copy-start(f32[1,16,1024]{2,1,0:T(8,128)} %param.15) | copy-start | bytes 196612
  59.2 5.7 %collective-permute-start.2 = (bf16[16,1024]{1,0:T(8,128)(2,1)S(1)}, bf16[16,1024]{1,0:T(8,128)(2,1)S(1)}, u32[]{:S(2)}, u32[]{:S(2)}) collective-permute-start(bf16[16,1024]{1,0:T(8,128)(2,1)S(1)} %get-tuple-element.102), channel_id=1, source_target_pairs={{0,4},{4,8},{8,12},{12,0},{1,5},{5,9},{9,13},{13,1},{2,6},{6,10},{... | collective-permute-start | bytes 98312 | tf_op jit(solution)/shard_map/ppermute | solution.py:13
  59.2 8.8 %collective-permute-start.3 = (bf16[16,1024]{1,0:T(8,128)(2,1)S(1)}, bf16[16,1024]{1,0:T(8,128)(2,1)S(1)}, u32[]{:S(2)}, u32[]{:S(2)}) collective-permute-start(bf16[16,1024]{1,0:T(8,128)(2,1)S(1)} %get-tuple-element.103), channel_id=1, source_target_pairs={{0,12},{4,0},{8,4},{12,8},{1,13},{5,1},{9,5},{13,9},{2,14},{6,2},{... | collective-permute-start | bytes 98312 | tf_op jit(solution)/shard_map/ppermute | solution.py:13
  114.9 3.9 %collective-permute-start.5 = (bf16[16,1024]{1,0:T(8,128)(2,1)S(1)}, bf16[16,1024]{1,0:T(8,128)(2,1)S(1)}, u32[]{:S(2)}, u32[]{:S(2)}) collective-permute-start(bf16[16,1024]{1,0:T(8,128)(2,1)S(1)} %get-tuple-element.100), channel_id=1, source_target_pairs={{0,12},{4,0},{8,4},{12,8},{1,13},{5,1},{9,5},{13,9},{2,14},{6,2},{... | collective-permute-start | bytes 98312 | tf_op jit(solution)/shard_map/ppermute | solution.py:13
  114.9 7.0 %collective-permute-start.4 = (bf16[16,1024]{1,0:T(8,128)(2,1)S(1)}, bf16[16,1024]{1,0:T(8,128)(2,1)S(1)}, u32[]{:S(2)}, u32[]{:S(2)}) collective-permute-start(bf16[16,1024]{1,0:T(8,128)(2,1)S(1)} %get-tuple-element.101), channel_id=1, source_target_pairs={{0,4},{4,8},{8,12},{12,0},{1,5},{5,9},{9,13},{13,1},{2,6},{6,10},{... | collective-permute-start | bytes 98312 | tf_op jit(solution)/shard_map/ppermute | solution.py:13
where the time goes:
time: 137 us; the launch traced here: 136 us
  blocking collectives  65.9 us (48%)
  matrix products  22.3 us (16%)
  local copies, waits for them, and re-layouts  22.1 us (16%)
  starting transfers between devices  11.4 us (8%)
  other arithmetic  8.41 us (6%)
  waiting for transfers between devices  3.74 us (3%)
  between operations  2.25 us (2%)
    psum x2, blocking collectives, apply_operator(): coarse = lax.psum(scattered, ('sub', 'row'))  37.5 us
    dot_general x16, matrix products, one_tile(): lax.dot_general(vector, piece, (((1,), (1,)), ((), ())), preferred_elemen...  20.7 us
    psum x2, blocking collectives, paired_totals(): lax.psum((inner(residual, precond, half), inner(precond, image, half)), '...  19.2 us
    ppermute x6, starting transfers between devices, shifted(): return lax.ppermute(value, axis, pairs)  11.4 us
    all_gather x2, blocking collectives, apply_operator(): lax.all_gather(united.astype(jnp.bfloat16), 'row', axis=1, tiled=True)  9.15 us
    gather x4, local copies, waits for them, and re-layouts, apply_operator(): jnp.take(arrived_right, right_map, axis=1)  5.95 us
    gather x4, local copies, waits for them, and re-layouts, apply_operator(): result_left = (lower + jnp.take(arrived_left, left_map, axis=1)) * live_left  5.95 us
    gather x1, local copies, waits for them, and re-layouts, per_device(): right_weight = jnp.take(received[1], right_map, axis=1)  4.53 us
  transfers between devices with their start and end apart: 6, of which 2 were waited for; matrix products, arithmetic and copies ran while one was open for 14% of the time, Pallas kernels for 0%

commit v1 on v0

--- a/solution.py
+++ b/solution.py
@@ -80,7 +80,7 @@
             own_slots, coupling, (((1,), (1,)), ((), ())), preferred_element_type=jnp.float32
         )
         scattered = jnp.dot(corner, own_hot, precision=lax.Precision.HIGHEST)
-        coarse = lax.psum(scattered, ("sub", "row"))
+        coarse = jnp.sum(lax.all_gather(scattered, ("sub", "row")), axis=0)
         solved = jnp.dot(coarse, coarse_inverse, precision=lax.Precision.HIGHEST)
         back = lax.dot_general(
             solved, own_hot, (((1,), (1,)), ((), ())), precision=lax.Precision.HIGHEST

time: 137 us -> 162 us (1.18)
  blocking collectives: 65.9 us -> 90.2 us
    all_gather x0 -> x2, blocking collectives: none -> 61.2 us  [apply_operator(): coarse = jnp.sum(lax.all_gather(scattered, ('sub', 'row')), axis=0)]
    psum x2 -> x0, blocking collectives: 37.5 us -> none  [apply_operator(): coarse = lax.psum(scattered, ('sub', 'row'))]
  transfers between devices with their start and end apart: 6 -> 6, of which waited for: 2 -> 2; matrix products, arithmetic and copies ran while one was open for 14% -> 12% of each run, Pallas kernels for 0% -> 0%
where the time goes in v1:
time: 162 us; the launch traced here: 160 us
  blocking collectives  90.2 us (56%)
  matrix products  22.3 us (14%)
  local copies, waits for them, and re-layouts  22.1 us (14%)
  starting transfers between devices  11.4 us (7%)
  other arithmetic  8.44 us (5%)
  waiting for transfers between devices  3.76 us (2%)
  between operations  2.23 us (1%)
    all_gather x2, blocking collectives, apply_operator(): coarse = jnp.sum(lax.all_gather(scattered, ('sub', 'row')), axis=0)  61.2 us
    dot_general x16, matrix products, one_tile(): lax.dot_general(vector, piece, (((1,), (1,)), ((), ())), preferred_elemen...  20.7 us
    psum x2, blocking collectives, paired_totals(): lax.psum((inner(residual, precond, half), inner(precond, image, half)), '...  19.8 us
    ppermute x6, starting transfers between devices, shifted(): return lax.ppermute(value, axis, pairs)  11.4 us
    all_gather x2, blocking collectives, apply_operator(): lax.all_gather(united.astype(jnp.bfloat16), 'row', axis=1, tiled=True)  9.15 us
    gather x4, local copies, waits for them, and re-layouts, apply_operator(): jnp.take(arrived_right, right_map, axis=1)  5.95 us
    gather x4, local copies, waits for them, and re-layouts, apply_operator(): result_left = (lower + jnp.take(arrived_left, left_map, axis=1)) * live_left  5.95 us
    gather x1, local copies, waits for them, and re-layouts, per_device(): right_weight = jnp.take(received[1], right_map, axis=1)  4.53 us
  transfers between devices with their start and end apart: 6, of which 2 were waited for; matrix products, arithmetic and copies ran while one was open for 12% of the time, Pallas kernels for 0%

profile of v1, /device:TPU:0, one launch (start us, length us, event | category | flops | bytes accessed | tf_op | source)
XLA Modules:
  0.0 160.5 jit_solution(12804455485948178169)
XLA Ops:
  0.7 0.9 bitcast_convert_fusion
  1.5 5.1 %collective-permute-start.1 = (bf16[16,1024]{1,0:T(8,128)(2,1)S(1)}, bf16[16,1024]{1,0:T(8,128)(2,1)S(1)}, u32[]{:S(2)}, u32[]{:S(2)}) collective-permute-start(bf16[16,1024]{1,0:T(8,128)(2,1)S(1)} %bitcast_convert_fusion), channel_id=1, source_target_pairs={{0,12},{4,0},{8,4},{12,8},{1,13},{5,1},{9,5},{13,9},{2,14},{6,2},{... | collective-permute-start | bytes 98312 | tf_op jit(solution)/shard_map/ppermute | solution.py:13
  6.6 0.7 convert_element_type.71
  7.3 0.4 collective-permute-start
  7.8 0.7 compare_select_fusion
  8.4 0.7 fusion.36
  9.1 1.3 fusion.49
  10.5 1.3 fusion.35
  11.8 1.3 compare_convert_fusion
  13.1 0.8 bitcast_multiply_fusion.1
  14.0 0.7 fusion.40
  14.7 0.7 fusion.37
  16.7 4.5 %gather_fusion = f32[1024]{0:T(1024)S(1)} fusion(f32[1024]{0:T(1024)S(1)} %bitcast.82, s32[1024]{0:T(1024)S(1)} %broadcast_clamp_fusion), kind=kCustom, calls=%fused_computation.5 | custom fusion | bytes 12288 | tf_op jit(solution)/shard_map/jit(_take)/gather | solution.py:105
  21.5 2.8 %gather_fusion.1 = f32[1024,16]{1,0:T(8,128)S(1)} fusion(f32[16,1024]{0,1:T(8,128)S(1)} %copy.21, s32[1024]{0:T(1024)S(1)} %fusion.36), kind=kCustom, calls=%fused_computation.clone | custom fusion | bytes 135168 | tf_op jit(solution)/shard_map/jit(_take)/gather | solution.py:104
  24.3 0.2 copy.22
  24.5 10.4 %while.20 = (s32[]{:T(128)}, f32[16,1024]{1,0:T(8,128)S(1)}, s32[]{:T(128)}, bf16[1024,2048]{1,0:T(8,128)(2,1)}, bf16[16,2048]{1,0:T(8,128)(2,1)S(1)}, /*index=5*/s32[]{:T(128)}, s32[]{:T(128)}, s32[]{:T(128)}, s32[]{:T(128)}) while((s32[]{:T(128)}, f32[16,1024]{1,0:T(8,128)S(1)}, s32[]{:T(128)}, bf16[1024,2048]{1,0:T(8,128)(2,1)}, ...), condition=%wide.region_3.5_spmd, body=%wide.region_2.4_spmd.sunk | while | flops 8388614 | bytes 599179 | solution.py:33
  24.6 1.3 fusion.72
  25.9 1.3 fusion.72
  27.1 1.3 fusion.72
  28.4 1.3 fusion.72
  29.7 1.3 fusion.72
  31.0 1.3 fusion.72
  32.3 1.3 fusion.72
  33.6 1.3 fusion.72
  34.9 0.1 fusion.25
  35.1 0.2 fusion.30
  35.3 30.6 %all-gather = f32[128,48]{1,0:T(8,128)S(1)} all-gather(f32[16,48]{1,0:T(8,128)S(1)} %fusion.30), channel_id=2, replica_groups=mesh['parts'=2,'sub'=4,'row'=2,'col'=2] {'sub','row'}, dimensions={0}, use_global_device_ids=true | all-gather | bytes 27648 | tf_op jit(solution)/shard_map/all_gather | solution.py:83
  66.0 0.2 convolution_convert_fusion.1
  66.2 0.1 fusion.6
  66.4 4.6 %all_gather.20 = bf16[16,2048]{1,0:T(8,128)(2,1)S(1)} all-gather(bf16[16,1024]{1,0:T(8,128)(2,1)S(1)} %fusion.6), channel_id=1, replica_groups=mesh['parts'=2,'sub'=4,'row'=2,'col'=2] {'row'}, dimensions={1}, use_global_device_ids=true | all-gather | bytes 98304 | tf_op jit(solution)/shard_map/all_gather | solution.py:89
  71.0 3.8 %collective-permute-start.3 = (bf16[16,1024]{1,0:T(8,128)(2,1)S(1)}, bf16[16,1024]{1,0:T(8,128)(2,1)S(1)}, u32[]{:S(2)}, u32[]{:S(2)}) collective-permute-start(bf16[16,1024]{1,0:T(8,128)(2,1)S(1)} %get-tuple-element.103), channel_id=1, source_target_pairs={{0,12},{4,0},{8,4},{12,8},{1,13},{5,1},{9,5},{13,9},{2,14},{6,2},{... | collective-permute-start | bytes 98312 | tf_op jit(solution)/shard_map/ppermute | solution.py:13
  74.8 1.9 %collective-permute-done.2 = bf16[16,1024]{1,0:T(8,128)(2,1)S(1)} collective-permute-done((bf16[16,1024]{1,0:T(8,128)(2,1)S(1)}, bf16[16,1024]{1,0:T(8,128)(2,1)S(1)}, u32[]{:S(2)}, u32[]{:S(2)}) %collective-permute-start.2) | collective-permute-done | bytes 32800 | tf_op jit(solution)/shard_map/ppermute | solution.py:13
  76.8 2.8 %gather_fusion.2 = f32[1024,16]{1,0:T(8,128)S(1)} fusion(f32[16,1024]{0,1:T(8,128)S(1)} %copy.23, s32[1024]{0:T(1024)S(1)} %fusion.37), kind=kCustom, calls=%fused_computation.1.clone | custom fusion | bytes 135168 | tf_op jit(solution)/shard_map/jit(_take)/gather | solution.py:96
  79.6 0.2 copy.24
  79.8 0.1 copy.25
  80.0 2.8 %gather_fusion.3 = f32[1024,16]{1,0:T(8,128)S(1)} fusion(f32[16,1024]{0,1:T(8,128)S(1)} %copy.25, s32[1024]{0:T(1024)S(1)} %fusion.36), kind=kCustom, calls=%fused_computation.2.clone | custom fusion | bytes 135168 | tf_op jit(solution)/shard_map/jit(_take)/gather | solution.py:97
  82.8 0.2 copy.26
  82.9 0.1 multiply_reduce_fusion.2
  83.1 9.0 %all-reduce.1 = (f32[16]{0:T(128)S(1)}, f32[16]{0:T(128)S(1)}) all-reduce(f32[16]{0:T(128)S(1)} %get-tuple-element.64, f32[16]{0:T(128)S(1)} %get-tuple-element.63), channel_id=1, replica_groups=mesh['parts'=2,'sub'=4,'row'=2,'col'=2] {'sub'}, use_global_device_ids=true, to_apply=%region_1.3 | all-reduce | flops 32 | bytes 256 | tf_op jit(solution)/shard_map/psum | solution.py:21
  92.4 10.3 %while.21 = (s32[]{:T(128)}, f32[16,1024]{1,0:T(8,128)S(1)}, s32[]{:T(128)}, bf16[1024,2048]{1,0:T(8,128)(2,1)}, bf16[16,2048]{1,0:T(8,128)(2,1)S(1)}, /*index=5*/s32[]{:T(128)}, s32[]{:T(128)}, s32[]{:T(128)}, s32[]{:T(128)}) while((s32[]{:T(128)}, f32[16,1024]{1,0:T(8,128)S(1)}, s32[]{:T(128)}, bf16[1024,2048]{1,0:T(8,128)(2,1)}, ...), condition=%wide.region_10.12_spmd, body=%wide.region_9.11_spmd.sunk | while | flops 8388614 | bytes 599179 | solution.py:33
  92.4 1.3 fusion.75
  93.7 1.3 fusion.75
  95.0 1.3 fusion.75
  96.2 1.3 fusion.75
  97.5 1.3 fusion.75
  98.8 1.3 fusion.75
  100.1 1.3 fusion.75
  101.4 1.3 fusion.75
  102.7 0.2 fusion.29
  102.9 30.6 %all-gather.1 = f32[128,48]{1,0:T(8,128)S(1)} all-gather(f32[16,48]{1,0:T(8,128)S(1)} %fusion.29), channel_id=3, replica_groups=mesh['parts'=2,'sub'=4,'row'=2,'col'=2] {'sub','row'}, dimensions={0}, use_global_device_ids=true | all-gather | bytes 27648 | tf_op jit(solution)/shard_map/all_gather | solution.py:83
  133.7 0.2 convolution_convert_fusion
  133.9 0.1 fusion.7
  134.0 4.6 %all_gather.23 = bf16[16,2048]{1,0:T(8,128)(2,1)S(1)} all-gather(bf16[16,1024]{1,0:T(8,128)(2,1)S(1)} %fusion.7), channel_id=1, replica_groups=mesh['parts'=2,'sub'=4,'row'=2,'col'=2] {'row'}, dimensions={1}, use_global_device_ids=true | all-gather | bytes 98304 | tf_op jit(solution)/shard_map/all_gather | solution.py:89
  138.6 0.6 collective-permute-start.5
  139.2 1.5 collective-permute-start.4
  140.7 1.9 %collective-permute-done.5 = bf16[16,1024]{1,0:T(8,128)(2,1)S(1)} collective-permute-done((bf16[16,1024]{1,0:T(8,128)(2,1)S(1)}, bf16[16,1024]{1,0:T(8,128)(2,1)S(1)}, u32[]{:S(2)}, u32[]{:S(2)}) %collective-permute-start.5) | collective-permute-done | bytes 32800 | tf_op jit(solution)/shard_map/ppermute | solution.py:13
  142.7 2.8 %gather_fusion.5 = f32[1024,16]{1,0:T(8,128)S(1)} fusion(f32[16,1024]{0,1:T(8,128)S(1)} %copy.29, s32[1024]{0:T(1024)S(1)} %fusion.36), kind=kCustom, calls=%fused_computation.4.clone | custom fusion | bytes 135168 | tf_op jit(solution)/shard_map/jit(_take)/gather | solution.py:97
  145.5 0.2 copy.30
  145.7 0.1 copy.27
  145.8 2.8 %gather_fusion.4 = f32[1024,16]{1,0:T(8,128)S(1)} fusion(f32[16,1024]{0,1:T(8,128)S(1)} %copy.27, s32[1024]{0:T(1024)S(1)} %fusion.37), kind=kCustom, calls=%fused_computation.3.clone | custom fusion | bytes 135168 | tf_op jit(solution)/shard_map/jit(_take)/gather | solution.py:96
  148.6 0.2 copy.28
  148.8 0.1 multiply_reduce_fusion
  149.0 10.8 %all-reduce = (f32[16]{0:T(128)S(1)}, f32[16]{0:T(128)S(1)}) all-reduce(f32[16]{0:T(128)S(1)} %get-tuple-element.62, f32[16]{0:T(128)S(1)} %get-tuple-element.61), channel_id=1, replica_groups=mesh['parts'=2,'sub'=4,'row'=2,'col'=2] {'sub'}, use_global_device_ids=true, to_apply=%region_8.10 | all-reduce | flops 32 | bytes 256 | tf_op jit(solution)/shard_map/psum | solution.py:21
  159.7 0.7 fusion.16
  (41 shorter events, 1.1 us)
Async XLA Ops:
  0.6 34.3 %copy-start = (bf16[1,24,1024]{2,1,0:T(8,128)(2,1)S(1)}, bf16[1,24,1024]{2,1,0:T(8,128)(2,1)}, u32[]{:S(2)}) copy-start(bf16[1,24,1024]{2,1,0:T(8,128)(2,1)} %param.18) | copy-start | bytes 147460
  0.6 20.7 %copy-start.5 = (f32[1,1024]{1,0:T(1,128)S(1)}, f32[1,1024]{1,0:T(1,128)}, u32[]{:S(2)}) copy-start(f32[1,1024]{1,0:T(1,128)} %param.16) | copy-start | bytes 12292
  0.7 20.6 %copy-start.2 = (s32[1,1024]{1,0:T(1,128)S(1)}, s32[1,1024]{1,0:T(1,128)}, u32[]{:S(2)}) copy-start(s32[1,1024]{1,0:T(1,128)} %param.23) | copy-start | bytes 12292
  1.5 19.8 %collective-permute-start.1 = (bf16[16,1024]{1,0:T(8,128)(2,1)S(1)}, bf16[16,1024]{1,0:T(8,128)(2,1)S(1)}, u32[]{:S(2)}, u32[]{:S(2)}) collective-permute-start(bf16[16,1024]{1,0:T(8,128)(2,1)S(1)} %bitcast_convert_fusion), channel_id=1, source_target_pairs={{0,12},{4,0},{8,4},{12,8},{1,13},{5,1},{9,5},{13,9},{2,14},{6,2},{... | collective-permute-start | bytes 98312 | tf_op jit(solution)/shard_map/ppermute | solution.py:13
  7.3 9.4 %collective-permute-start = (bf16[1,1024]{1,0:T(2,128)(2,1)S(1)}, bf16[1,1024]{1,0:T(2,128)(2,1)S(1)}, u32[]{:S(2)}, u32[]{:S(2)}) collective-permute-start(bf16[1,1024]{1,0:T(2,128)(2,1)S(1)} %convert_element_type.71), channel_id=1, source_target_pairs={{0,12},{4,0},{8,4},{12,8},{1,13},{5,1},{9,5},{13,9},{2,14},{6,2},{... | collective-permute-start | bytes 6152 | tf_op jit(solution)/shard_map/ppermute | solution.py:13
  16.7 49.1 %copy-start.3 = (f32[48,48]{1,0:T(8,128)S(1)}, f32[48,48]{1,0:T(8,128)}, u32[]{:S(2)}) copy-start(f32[48,48]{1,0:T(8,128)} %param.19) | copy-start | bytes 27652
  21.3 53.5 %copy-start.4 = (s32[1,1024]{1,0:T(1,128)S(1)}, s32[1,1024]{1,0:T(1,128)}, u32[]{:S(2)}) copy-start(s32[1,1024]{1,0:T(1,128)} %param.22) | copy-start | bytes 12292
  24.5 58.5 %copy-start.1 = (f32[1,16,1024]{2,1,0:T(8,128)S(1)}, f32[1,16,1024]{2,1,0:T(8,128)}, u32[]{:S(2)}) copy-start(f32[1,16,1024]{2,1,0:T(8,128)} %param.15) | copy-start | bytes 196612
  70.9 5.7 %collective-permute-start.2 = (bf16[16,1024]{1,0:T(8,128)(2,1)S(1)}, bf16[16,1024]{1,0:T(8,128)(2,1)S(1)}, u32[]{:S(2)}, u32[]{:S(2)}) collective-permute-start(bf16[16,1024]{1,0:T(8,128)(2,1)S(1)} %get-tuple-element.102), channel_id=1, source_target_pairs={{0,4},{4,8},{8,12},{12,0},{1,5},{5,9},{9,13},{13,1},{2,6},{6,10},{... | collective-permute-start | bytes 98312 | tf_op jit(solution)/shard_map/ppermute | solution.py:13
  71.0 8.8 %collective-permute-start.3 = (bf16[16,1024]{1,0:T(8,128)(2,1)S(1)}, bf16[16,1024]{1,0:T(8,128)(2,1)S(1)}, u32[]{:S(2)}, u32[]{:S(2)}) collective-permute-start(bf16[16,1024]{1,0:T(8,128)(2,1)S(1)} %get-tuple-element.103), channel_id=1, source_target_pairs={{0,12},{4,0},{8,4},{12,8},{1,13},{5,1},{9,5},{13,9},{2,14},{6,2},{... | collective-permute-start | bytes 98312 | tf_op jit(solution)/shard_map/ppermute | solution.py:13
  138.6 3.9 %collective-permute-start.5 = (bf16[16,1024]{1,0:T(8,128)(2,1)S(1)}, bf16[16,1024]{1,0:T(8,128)(2,1)S(1)}, u32[]{:S(2)}, u32[]{:S(2)}) collective-permute-start(bf16[16,1024]{1,0:T(8,128)(2,1)S(1)} %get-tuple-element.100), channel_id=1, source_target_pairs={{0,12},{4,0},{8,4},{12,8},{1,13},{5,1},{9,5},{13,9},{2,14},{6,2},{... | collective-permute-start | bytes 98312 | tf_op jit(solution)/shard_map/ppermute | solution.py:13
  139.2 6.5 %collective-permute-start.4 = (bf16[16,1024]{1,0:T(8,128)(2,1)S(1)}, bf16[16,1024]{1,0:T(8,128)(2,1)S(1)}, u32[]{:S(2)}, u32[]{:S(2)}) collective-permute-start(bf16[16,1024]{1,0:T(8,128)(2,1)S(1)} %get-tuple-element.101), channel_id=1, source_target_pairs={{0,4},{4,8},{8,12},{12,0},{1,5},{5,9},{9,13},{13,1},{2,6},{6,10},{... | collective-permute-start | bytes 98312 | tf_op jit(solution)/shard_map/ppermute | solution.py:13
